TPU v7x, 32 devices: a whole 2x2x4 slice. The times are simulated.
32 devices in a mesh: groups: 2 (over x), tier: 16 (over z, y, core).
Axes of the slice: x: 2, y: 2, z: 4, core: 2. Of those that a mesh axis runs over, the one named last changes fastest.
Arguments:
- rho: float32 [256, 2, 256, 256], P(('groups', 'tier')), parts along dimension 0, may hold values from -6 to 6
- hamiltonian: float32 [256, 256], replicated, may hold values from -0.375 to 0.375
- couplings: float32 [4, 256, 256], replicated, may hold values from -0.375 to 0.375
- bath_coef: float32 [8, 2], P('groups'), parts along dimension 0, may hold values from 0.3 to 1.5
- damping: float32 [256], P(('groups', 'tier')), parts along dimension 0, may hold values from 0.2 to 3
- match_edges: int32 [16, 4, 1, 5], P('tier'), may hold values from 0 to 7, as said below
- left_rows: int32 [16, 6, 5], replicated, may hold values from 0 to 127, as said below
- left_count: int32 [16], replicated, may hold values from 1 to 6, as said below
Outputs:
- rho_next: float32 [256, 2, 256, 256], P(('groups', 'tier')), parts along dimension 0
There are 2 independent parts, one for each index of `groups`. A program takes and returns all parts, laid end to end along the dimension named above; an argument that names none is the same for every part. Nothing has to cross between parts.
Inputs may be any that keep to these rules, and one draw needn't show every extreme that they name: match_edges[b, c, j] = (target slot, partner slot, mode, lower flag 0 or 1, occupation 1 to 3); the row (b XOR 2^c, c, j) describes the same edge from the partner's side: its target slot is this row's partner slot and the reverse, same mode and occupation, opposite lower flag. left_rows[b, j] = (target slot, source matrix index, mode, lower flag 0 or 1, occupation 1 to 3); the source's block lies at cyclic block distance 1 to 4 from b, and the rows of one block name distinct source blocks. Only the first left_count[b] rows of block b are live; some block has exactly 6.
All inputs are finite; a program needn't handle non-finite values.
Results may differ from a plain program's by a relative error of at most 0.00005.
Values sent between devices are 32-bit elements; how exact they have to be, the bound alone decides.
A program may use at most 128 MiB of HBM per device.

v0:
```python
import functools

import jax
import jax.numpy as jnp
from jax import lax
from jax.experimental import pallas as pl
from jax.experimental.pallas import tpu as pltpu
from jax.sharding import PartitionSpec as P

REACH = 4
STEP = 0.1
F32 = jnp.float32
BF16 = jnp.bfloat16


def split(value):
    high = value.astype(BF16)
    low = (value - high.astype(F32)).astype(BF16)
    return high, low


def flip(index, stride):
    return index + stride - 2 * stride * ((index // stride) % 2)


def kernel(
    tier_size,
    colours,
    rho_ref,
    ham_ref,
    coup_ref,
    bath_ref,
    damp_ref,
    match_ref,
    left_ref,
    count_ref,
    out_ref,
    first_ref,
    term_ref,
    packed,
    arrived,
    op_left,
    op_right,
    send_sem,
    recv_sem,
):
    me = lax.axis_index("tier")
    mats = rho_ref.shape[0]
    order = rho_ref.shape[2]
    modes = coup_ref.shape[0]
    left_cap = left_ref.shape[1]
    deltas = [d for d in range(-REACH, 0)] + [d for d in range(1, REACH + 1)]
    rows = colours + len(deltas)

    targets = [flip(me, 2**c) for c in range(colours)]
    targets += [lax.rem(me - d + tier_size, tier_size) for d in deltas]

    barrier = pltpu.get_barrier_semaphore()
    for device in targets:
        pl.semaphore_signal(barrier, inc=1, device_id={"tier": device}, device_id_type=pl.DeviceIdType.MESH)
    pl.semaphore_wait(barrier, rows)

    def asked_slot(delta):
        asker = lax.rem(me - delta + tier_size, tier_size)
        slot = jnp.int32(0)
        for j in range(left_cap):
            source = left_ref[asker, j, 1]
            hit = (source // mats == me) & (j < count_ref[asker])
            slot = jnp.where(hit, source % mats, slot)
        return slot

    slots = [match_ref[c, 0] for c in range(colours)] + [asked_slot(d) for d in deltas]

    def copies(stage):
        return [
            pltpu.make_async_remote_copy(
                src_ref=packed.at[i],
                dst_ref=arrived.at[stage, i],
                send_sem=send_sem.at[stage, i],
                recv_sem=recv_sem.at[stage, i],
                device_id={"tier": targets[i]},
                device_id_type=pl.DeviceIdType.MESH,
            )
            for i in range(rows)
        ]

    def products(value, left, right):
        re_high, re_low = split(value[0])
        im_high, im_low = split(value[1])
        column = jnp.concatenate(
            [
                jnp.concatenate([re_high, re_low, re_high], axis=0),
                jnp.concatenate([im_high, im_low, im_high], axis=0),
            ],
            axis=1,
        )
        row = jnp.concatenate(
            [
                jnp.concatenate([re_high, re_low, re_high], axis=1),
                jnp.concatenate([im_high, im_low, im_high], axis=1),
            ],
            axis=0,
        )
        p = jnp.dot(left, column, preferred_element_type=F32)
        r = jnp.dot(row, right, preferred_element_type=F32)
        return p[:, :order], p[:, order:], r[:order], r[order:]

    def row_facts(i):
        c = jnp.minimum(i, colours - 1)
        is_match = i < colours
        q = i - colours
        delta = jnp.where(q < REACH, q - REACH, q - REACH + 1)
        source = lax.rem(me + delta + tier_size, tier_size)
        target, mode, flag, occ, weight = jnp.int32(0), jnp.int32(0), jnp.int32(0), jnp.int32(0), jnp.int32(0)
        for j in range(left_cap):
            hit = (left_ref[me, j, 1] // mats == source) & (j < count_ref[me])
            target = jnp.where(hit, left_ref[me, j, 0], target)
            mode = jnp.where(hit, left_ref[me, j, 2], mode)
            flag = jnp.where(hit, left_ref[me, j, 3], flag)
            occ = jnp.where(hit, left_ref[me, j, 4], occ)
            weight = jnp.where(hit, 1, weight)
        target = jnp.where(is_match, match_ref[c, 0], target)
        mode = jnp.where(is_match, match_ref[c, 2], mode)
        flag = jnp.where(is_match, match_ref[c, 3], flag)
        occ = jnp.where(is_match, match_ref[c, 4], occ)
        weight = jnp.where(is_match, 1, weight)
        a = jnp.where(flag == 1, F32(1.0), bath_ref[mode, 0])
        b = jnp.where(flag == 1, F32(0.0), bath_ref[mode, 1])
        return target, mode, a, b, occ, weight

    def handle_row(i, stage, scale, acc):
        pltpu.make_async_remote_copy(
            src_ref=packed.at[i],
            dst_ref=arrived.at[stage, i],
            send_sem=send_sem.at[stage, i],
            recv_sem=recv_sem.at[stage, i],
            device_id={"tier": targets[0]},
            device_id_type=pl.DeviceIdType.MESH,
        ).wait_recv()
        target, mode, a, b, occ, weight = row_facts(i)
        p_re, p_im, r_re, r_im = products(arrived[stage, i], op_left[mode], op_right[mode])
        root = jnp.sqrt(jnp.full((1, order), occ, jnp.int32).astype(F32)) * weight.astype(F32) * scale
        ca = root * a
        cb = root * b
        term_ref[0] = ca * (p_im - r_im) + cb * (p_re + r_re)
        term_ref[1] = cb * (p_im + r_im) - ca * (p_re - r_re)

        def add(s, carry):
            chosen = jnp.where(target == s, F32(1.0), F32(0.0))
            acc[s] = acc[s] + chosen * term_ref[...]
            return carry

        lax.fori_loop(0, mats, add, 0)

    def pack(source):
        for i in range(rows):
            packed[i] = source[slots[i]]

    pack(rho_ref)
    sends = copies(0)
    for copy in sends:
        copy.start()

    def prepare(k, carry):
        high, low = split(coup_ref[k])
        op_left[k] = jnp.concatenate([high, high, low], axis=1)
        op_right[k] = jnp.concatenate([high, high, low], axis=0)
        return carry

    lax.fori_loop(0, modes, prepare, 0)
    high, low = split(ham_ref[...])
    op_left[modes] = jnp.concatenate([high, high, low], axis=1)
    op_right[modes] = jnp.concatenate([high, high, low], axis=0)

    def own(n, carry):
        value = rho_ref[n]
        p_re, p_im, r_re, r_im = products(value, op_left[modes], op_right[modes])
        first_ref[n, 0] = (p_im - r_im) - damp_ref[n] * value[0]
        first_ref[n, 1] = (r_re - p_re) - damp_ref[n] * value[1]
        return carry

    lax.fori_loop(0, mats, own, 0)

    def row_first(i, carry):
        handle_row(i, 0, F32(1.0), first_ref)
        return carry

    lax.fori_loop(0, rows, row_first, 0)
    for copy in sends:
        copy.wait_send()

    pack(first_ref)
    sends = copies(1)
    for copy in sends:
        copy.start()

    half = F32(0.5 * STEP * STEP)

    def own_second(n, carry):
        value = first_ref[n]
        p_re, p_im, r_re, r_im = products(value, op_left[modes], op_right[modes])
        out_ref[n, 0] = rho_ref[n, 0] + F32(STEP) * value[0] + half * ((p_im - r_im) - damp_ref[n] * value[0])
        out_ref[n, 1] = rho_ref[n, 1] + F32(STEP) * value[1] + half * ((r_re - p_re) - damp_ref[n] * value[1])
        return carry

    lax.fori_loop(0, mats, own_second, 0)

    def row_second(i, carry):
        handle_row(i, 1, half, out_ref)
        return carry

    lax.fori_loop(0, rows, row_second, 0)
    for copy in sends:
        copy.wait_send()


def body(tier_size, rho, hamiltonian, couplings, bath_coef, damping, match_edges, left_rows, left_count):
    mats, _, order, _ = rho.shape
    modes = couplings.shape[0]
    table = match_edges.reshape(-1, match_edges.shape[-1])
    colours = table.shape[0]
    rows = colours + 2 * REACH
    vmem = pl.BlockSpec(memory_space=pltpu.VMEM)
    smem = pl.BlockSpec(memory_space=pltpu.SMEM)
    return pl.pallas_call(
        functools.partial(kernel, tier_size, colours),
        out_shape=jax.ShapeDtypeStruct(rho.shape, F32),
        in_specs=[vmem, vmem, vmem, smem, smem, smem, smem, smem],
        out_specs=vmem,
        scratch_shapes=[
            pltpu.VMEM(rho.shape, F32),
            pltpu.VMEM((2, order, order), F32),
            pltpu.VMEM((rows, 2, order, order), F32),
            pltpu.VMEM((2, rows, 2, order, order), F32),
            pltpu.VMEM((modes + 1, order, 3 * order), BF16),
            pltpu.VMEM((modes + 1, 3 * order, order), BF16),
            pltpu.SemaphoreType.DMA((2, rows)),
            pltpu.SemaphoreType.DMA((2, rows)),
        ],
        compiler_params=pltpu.CompilerParams(
            collective_id=0, has_side_effects=True, vmem_limit_bytes=60 * 1024 * 1024
        ),
    )(rho, hamiltonian, couplings, bath_coef, damping, table, left_rows, left_count)


def solution(mesh):
    placed = (
        P(("groups", "tier"), None, None, None),
        P(),
        P(),
        P("groups", None),
        P(("groups", "tier")),
        P("tier", None, None, None),
        P(),
        P(),
    )
    return jax.shard_map(
        functools.partial(body, mesh.shape["tier"]),
        mesh=mesh,
        in_specs=placed,
        out_specs=P(("groups", "tier"), None, None, None),
        check_vma=False,
    )
```

profile of v0, /device:TPU:16, one launch (start us, length us, event | category | flops | bytes accessed | tf_op | source)
XLA Modules:
  0.0 180.7 jit_solution(15993409458139466789)
XLA Ops:
  0.0 1.3 copy.9.bath_ref
  1.3 1.5 copy.10.left_ref
  2.8 173.2 %shard_map.82 = f32[8,2,256,256]{3,2,1,0:T(8,128)} custom-call(f32[8,2,256,256]{3,2,1,0:T(8,128)} %rho_ref.1, f32[256,256]{1,0:T(8,128)} %ham_ref.1, f32[4,256,256]{2,1,0:T(8,128)} %coup_ref.1, f32[4,2]{1,0:T(4,128)} %copy.9.bath_ref, f32[8]{0:T(128)} %damp_ref.1, s32[4,5]{1,0:T(4,128)} %bitcast.1, s32[16,6,5]{2,1,0:T(8,128)} %copy.10.left_ref, s32[16]{0:T(128)} %count_ref.1), custom_call_target="tpu_custom_call" | custom-call | tf_op jit(solution)/shard_map/pallas_call | solution.py:225
  176.1 4.6 %copy.12 = f32[8,2,256,256]{3,2,1,0:T(8,128)} copy(f32[8,2,256,256]{3,2,1,0:T(8,128)} %shard_map.82) | data formatting | bytes 8388608
where the time goes:
time: 181 us
  Pallas kernels  173 us (96%)
  local copies, waits for them, and re-layouts  7.41 us (4%)
    pallas_call x1, Pallas kernels, body(): pl.pallas_call(functools.partial(kernel, tier_size, colours), out_shape=j...  173 us
    unnamed x3, local copies, waits for them, and re-layouts  7.41 us

commit v1 on v0

--- a/solution.py
+++ b/solution.py
@@ -26,7 +26,7 @@
 def kernel(
     tier_size,
     colours,
-    rho_ref,
+    rho_any,
     ham_ref,
     coup_ref,
     bath_ref,
@@ -35,6 +35,8 @@
     left_ref,
     count_ref,
     out_ref,
+    rho_ref,
+    rho_sem,
     first_ref,
     term_ref,
     packed,
@@ -44,6 +46,8 @@
     send_sem,
     recv_sem,
 ):
+    load = pltpu.make_async_copy(rho_any, rho_ref, rho_sem)
+    load.start()
     me = lax.axis_index("tier")
     mats = rho_ref.shape[0]
     order = rho_ref.shape[2]
@@ -64,7 +68,7 @@
         asker = lax.rem(me - delta + tier_size, tier_size)
         slot = jnp.int32(0)
         for j in range(left_cap):
-            source = left_ref[asker, j, 1]
+            source = left_ref[1, j, asker]
             hit = (source // mats == me) & (j < count_ref[asker])
             slot = jnp.where(hit, source % mats, slot)
         return slot
@@ -113,19 +117,19 @@
         source = lax.rem(me + delta + tier_size, tier_size)
         target, mode, flag, occ, weight = jnp.int32(0), jnp.int32(0), jnp.int32(0), jnp.int32(0), jnp.int32(0)
         for j in range(left_cap):
-            hit = (left_ref[me, j, 1] // mats == source) & (j < count_ref[me])
-            target = jnp.where(hit, left_ref[me, j, 0], target)
-            mode = jnp.where(hit, left_ref[me, j, 2], mode)
-            flag = jnp.where(hit, left_ref[me, j, 3], flag)
-            occ = jnp.where(hit, left_ref[me, j, 4], occ)
+            hit = (left_ref[1, j, me] // mats == source) & (j < count_ref[me])
+            target = jnp.where(hit, left_ref[0, j, me], target)
+            mode = jnp.where(hit, left_ref[2, j, me], mode)
+            flag = jnp.where(hit, left_ref[3, j, me], flag)
+            occ = jnp.where(hit, left_ref[4, j, me], occ)
             weight = jnp.where(hit, 1, weight)
         target = jnp.where(is_match, match_ref[c, 0], target)
         mode = jnp.where(is_match, match_ref[c, 2], mode)
         flag = jnp.where(is_match, match_ref[c, 3], flag)
         occ = jnp.where(is_match, match_ref[c, 4], occ)
         weight = jnp.where(is_match, 1, weight)
-        a = jnp.where(flag == 1, F32(1.0), bath_ref[mode, 0])
-        b = jnp.where(flag == 1, F32(0.0), bath_ref[mode, 1])
+        a = jnp.where(flag == 1, F32(1.0), bath_ref[0, mode])
+        b = jnp.where(flag == 1, F32(0.0), bath_ref[1, mode])
         return target, mode, a, b, occ, weight
 
     def handle_row(i, stage, scale, acc):
@@ -152,14 +156,17 @@
 
         lax.fori_loop(0, mats, add, 0)
 
-    def pack(source):
+    def pack_and_send(source, stage):
+        sends = copies(stage)
         for i in range(rows):
             packed[i] = source[slots[i]]
-
-    pack(rho_ref)
-    sends = copies(0)
-    for copy in sends:
-        copy.start()
+            if i > 0:
+                sends[i - 1].start()
+        sends[rows - 1].start()
+        return sends
+
+    load.wait()
+    sends = pack_and_send(rho_ref, 0)
 
     def prepare(k, carry):
         high, low = split(coup_ref[k])
@@ -189,10 +196,7 @@
     for copy in sends:
         copy.wait_send()
 
-    pack(first_ref)
-    sends = copies(1)
-    for copy in sends:
-        copy.start()
+    sends = pack_and_send(first_ref, 1)
 
     half = F32(0.5 * STEP * STEP)
 
@@ -224,10 +228,12 @@
     smem = pl.BlockSpec(memory_space=pltpu.SMEM)
     return pl.pallas_call(
         functools.partial(kernel, tier_size, colours),
-        out_shape=jax.ShapeDtypeStruct(rho.shape, F32),
-        in_specs=[vmem, vmem, vmem, smem, smem, smem, smem, smem],
+        out_shape=pltpu.VMEM(rho.shape, F32),
+        in_specs=[pl.BlockSpec(memory_space=pl.ANY), vmem, vmem, smem, smem, smem, smem, smem],
         out_specs=vmem,
         scratch_shapes=[
+            pltpu.VMEM(rho.shape, F32),
+            pltpu.SemaphoreType.DMA,
             pltpu.VMEM(rho.shape, F32),
             pltpu.VMEM((2, order, order), F32),
             pltpu.VMEM((rows, 2, order, order), F32),
@@ -238,9 +244,9 @@
             pltpu.SemaphoreType.DMA((2, rows)),
         ],
         compiler_params=pltpu.CompilerParams(
-            collective_id=0, has_side_effects=True, vmem_limit_bytes=60 * 1024 * 1024
+            collective_id=0, has_side_effects=True, vmem_limit_bytes=50 * 1024 * 1024
         ),
-    )(rho, hamiltonian, couplings, bath_coef, damping, table, left_rows, left_count)
+    )(rho, hamiltonian, couplings, bath_coef.T, damping, table, left_rows.transpose(2, 1, 0), left_count)
 
 
 def solution(mesh):

time: 181 us -> 172 us (0.950)
  local copies, waits for them, and re-layouts: 7.41 us -> 2.02 us
  Pallas kernels: 173 us -> 169 us
    unnamed x3 -> x1, local copies, waits for them, and re-layouts: 7.41 us -> 2.02 us
    pallas_call x1, Pallas kernels: 173 us -> 169 us  [body(): pl.pallas_call(functools.partial(kernel, tier_size, colours), out_shape=p...]
where the time goes in v1:
time: 172 us; the launch traced here: 171 us
  Pallas kernels  169 us (98%)
  local copies, waits for them, and re-layouts  2.02 us (1%)
    pallas_call x1, Pallas kernels, body(): pl.pallas_call(functools.partial(kernel, tier_size, colours), out_shape=p...  169 us

profile of v1, /device:TPU:16, one launch (start us, length us, event | category | flops | bytes accessed | tf_op | source)
XLA Modules:
  0.0 171.5 jit_solution(7720964174685143174)
XLA Ops:
  0.0 169.4 %shard_map.82 = f32[8,2,256,256]{3,2,1,0:T(8,128)S(1)} custom-call(f32[8,2,256,256]{3,2,1,0:T(8,128)} %rho_any.1, f32[256,256]{1,0:T(8,128)} %ham_ref.1, f32[4,256,256]{2,1,0:T(8,128)} %coup_ref.1, f32[2,4]{1,0:T(2,128)} %bitcast.5, f32[8]{0:T(128)} %damp_ref.1, s32[4,5]{1,0:T(4,128)} %bitcast.4, s32[5,6,16]{2,1,0:T(8,128)} %bitcast.3, s32[16]{0:T(128)} %count_ref.1), custom_call_target="tpu_custom_call" | custom-call | tf_op jit(solution)/shard_map/pallas_call | solution.py:229
  169.4 2.0 %copy.10 = f32[8,2,256,256]{3,2,1,0:T(8,128)} copy(f32[8,2,256,256]{3,2,1,0:T(8,128)S(1)} %shard_map.82) | data formatting | bytes 8388608

commit v2 on v1

--- a/solution.py
+++ b/solution.py
@@ -27,8 +27,8 @@
     tier_size,
     colours,
     rho_any,
-    ham_ref,
-    coup_ref,
+    ham_any,
+    coup_any,
     bath_ref,
     damp_ref,
     match_ref,
@@ -36,7 +36,9 @@
     count_ref,
     out_ref,
     rho_ref,
-    rho_sem,
+    ham_ref,
+    coup_ref,
+    load_sem,
     first_ref,
     term_ref,
     packed,
@@ -46,14 +48,19 @@
     send_sem,
     recv_sem,
 ):
-    load = pltpu.make_async_copy(rho_any, rho_ref, rho_sem)
-    load.start()
+    loads = [
+        pltpu.make_async_copy(rho_any, rho_ref, load_sem.at[0]),
+        pltpu.make_async_copy(ham_any, ham_ref, load_sem.at[1]),
+        pltpu.make_async_copy(coup_any, coup_ref, load_sem.at[2]),
+    ]
+    for load in loads:
+        load.start()
     me = lax.axis_index("tier")
     mats = rho_ref.shape[0]
     order = rho_ref.shape[2]
     modes = coup_ref.shape[0]
     left_cap = left_ref.shape[1]
-    deltas = [d for d in range(-REACH, 0)] + [d for d in range(1, REACH + 1)]
+    deltas = [d for d in range(REACH, 0, -1)] + [d for d in range(-1, -REACH - 1, -1)]
     rows = colours + len(deltas)
 
     targets = [flip(me, 2**c) for c in range(colours)]
@@ -113,7 +120,7 @@
         c = jnp.minimum(i, colours - 1)
         is_match = i < colours
         q = i - colours
-        delta = jnp.where(q < REACH, q - REACH, q - REACH + 1)
+        delta = jnp.where(q < REACH, REACH - q, REACH - 1 - q)
         source = lax.rem(me + delta + tier_size, tier_size)
         target, mode, flag, occ, weight = jnp.int32(0), jnp.int32(0), jnp.int32(0), jnp.int32(0), jnp.int32(0)
         for j in range(left_cap):
@@ -165,8 +172,10 @@
         sends[rows - 1].start()
         return sends
 
-    load.wait()
+    loads[0].wait()
     sends = pack_and_send(rho_ref, 0)
+    loads[1].wait()
+    loads[2].wait()
 
     def prepare(k, carry):
         high, low = split(coup_ref[k])
@@ -225,15 +234,18 @@
     colours = table.shape[0]
     rows = colours + 2 * REACH
     vmem = pl.BlockSpec(memory_space=pltpu.VMEM)
+    hbm = pl.BlockSpec(memory_space=pl.ANY)
     smem = pl.BlockSpec(memory_space=pltpu.SMEM)
     return pl.pallas_call(
         functools.partial(kernel, tier_size, colours),
         out_shape=pltpu.VMEM(rho.shape, F32),
-        in_specs=[pl.BlockSpec(memory_space=pl.ANY), vmem, vmem, smem, smem, smem, smem, smem],
+        in_specs=[hbm, hbm, hbm, smem, smem, smem, smem, smem],
         out_specs=vmem,
         scratch_shapes=[
             pltpu.VMEM(rho.shape, F32),
-            pltpu.SemaphoreType.DMA,
+            pltpu.VMEM(hamiltonian.shape, F32),
+            pltpu.VMEM(couplings.shape, F32),
+            pltpu.SemaphoreType.DMA((3,)),
             pltpu.VMEM(rho.shape, F32),
             pltpu.VMEM((2, order, order), F32),
             pltpu.VMEM((rows, 2, order, order), F32),

time: 172 us -> 171 us (level)
  the two profiles are of different devices: /device:TPU:16 before, /device:TPU:1 now
where the time goes in v2:
time: 171 us
  Pallas kernels  169 us (99%)
  local copies, waits for them, and re-layouts  2.02 us (1%)
    pallas_call x1, Pallas kernels, body(): pl.pallas_call(functools.partial(kernel, tier_size, colours), out_shape=p...  169 us

profile of v2, /device:TPU:1, one launch (start us, length us, event | category | flops | bytes accessed | tf_op | source)
XLA Modules:
  0.0 170.7 jit_solution(12137388400223671506)
XLA Ops:
  0.0 168.6 %shard_map.82 = f32[8,2,256,256]{3,2,1,0:T(8,128)S(1)} custom-call(f32[8,2,256,256]{3,2,1,0:T(8,128)} %rho_any.1, f32[256,256]{1,0:T(8,128)} %ham_any.1, f32[4,256,256]{2,1,0:T(8,128)} %coup_any.1, f32[2,4]{1,0:T(2,128)} %bitcast.5, f32[8]{0:T(128)} %damp_ref.1, s32[4,5]{1,0:T(4,128)} %bitcast.4, s32[5,6,16]{2,1,0:T(8,128)} %bitcast.3, s32[16]{0:T(128)} %count_ref.1), custom_call_target="tpu_custom_call" | custom-call | tf_op jit(solution)/shard_map/pallas_call | solution.py:239
  168.7 2.0 %copy.10 = f32[8,2,256,256]{3,2,1,0:T(8,128)} copy(f32[8,2,256,256]{3,2,1,0:T(8,128)S(1)} %shard_map.82) | data formatting | bytes 8388608
